TPU v7x, 32 devices: a whole 2x2x4 slice. The times are simulated.
32 devices in a mesh: req: 8 (over z, x), mlp: 4 (over y, core).
Axes of the slice: x: 2, y: 2, z: 4, core: 2. Of those that a mesh axis runs over, the one named last changes fastest.
Arguments:
- tokens: bfloat16 [8192, 2048], P('req', 'mlp'), may hold values from -40 to 40, as said below
- norm_gain_vector: bfloat16 [2048], replicated, may hold values from 0.099609375 to 1.8984375
- gate_weight: bfloat16 [2048, 3584], P(None, 'mlp'), may hold values from -0.125 to 0.125
- up_weight: bfloat16 [2048, 3584], P(None, 'mlp'), may hold values from -0.125 to 0.125
- down_weight: bfloat16 [3584, 2048], P('mlp'), may hold values from -0.09375 to 0.09375
- gate_up_input_maps: bfloat16 [8, 2048, 32], P('req'), may hold values from -0.125 to 0.125
- gate_up_output_maps: bfloat16 [8, 2, 16, 3584], P('req', None, None, 'mlp'), may hold values from -1.5 to 1.5
- down_input_maps: bfloat16 [8, 3584, 16], P('req', 'mlp'), may hold values from -0.09375 to 0.09375
- down_output_maps: bfloat16 [8, 16, 2048], P('req'), may hold values from -1.5 to 1.5
- lengths: int32 [8, 4], replicated, may hold values from 0 to 1024, as said below
- request_adapter_slot: int32 [8, 4], replicated, may hold values from 0 to 7
- selected: int32 [8], replicated, may hold values from 0 to 7, as said below
Outputs:
- layer_out: bfloat16 [8192, 2048], P('req', 'mlp')
Inputs may be any that keep to these rules, and one draw needn't show every extreme that they name: Each row of lengths sums to a multiple of 64 from 64 to 1024; some row sums to exactly 1024 and holds all of it in one slot; all rows together sum to 4096. Slots may hold zero tokens. `selected`: 8 different adapter ids; adapter a is owned by index a // 1 of req. `tokens`: entries of order one, some rows and features larger than others.
All inputs are finite; a program needn't handle non-finite values.
Results may differ from a plain program's by a relative error of at most 0.006.
Values may be sent and summed in bfloat16 or wider, within the bound.
A program may use at most 128 MiB of HBM per device.

v0:
```python
import jax
import jax.numpy as jnp
from jax import lax
from jax.sharding import PartitionSpec as P

TOK_DEV = 512


EPSILON = 1e-06


def gather_adapter_maps(gate_up_input_maps, gate_up_output_maps, down_input_maps, down_output_maps):
    token_count = gate_up_input_maps.shape[0]
    return jnp.concatenate(
        [
            gate_up_input_maps.reshape(token_count, -1),
            gate_up_output_maps.reshape(token_count, -1),
            down_input_maps.reshape(token_count, -1),
            down_output_maps.reshape(token_count, -1),
        ],
        axis=1,
    )


def unpack_adapters(packed_adapters, width_size, rank_size, inner_hidden):
    token_count = packed_adapters.shape[0]
    first_branch = width_size * 2 * rank_size
    second_branch = first_branch + 2 * rank_size * inner_hidden
    third = second_branch + inner_hidden * rank_size
    gate_up_input_maps = packed_adapters[:, :first_branch].reshape(
        token_count, width_size, 2 * rank_size
    )
    gate_up_output_maps = packed_adapters[:, first_branch:second_branch].reshape(
        token_count, 2, rank_size, inner_hidden
    )
    down_input_maps = packed_adapters[:, second_branch:third].reshape(
        token_count, inner_hidden, rank_size
    )
    down_output_maps = packed_adapters[:, third:].reshape(token_count, rank_size, width_size)
    return (gate_up_input_maps, gate_up_output_maps, down_input_maps, down_output_maps)


def slot_table(owners, positions, lengths, request_adapter_slot, token_count):
    lens = jnp.take(lengths, owners, axis=0)
    req_ends = jnp.cumsum(lens, axis=1)
    starts = req_ends - lens
    inside = (positions[:, None] >= starts) & (positions[:, None] < req_ends)
    adapter_ids = jnp.take(request_adapter_slot, owners, axis=0)
    picked = jnp.sum(jnp.where(inside, adapter_ids, 0), axis=1)
    live = jnp.any(inside, axis=1)
    onehot = (picked[:, None] == jnp.arange(token_count, dtype=jnp.int32)[None, :]) & live[:, None]
    return onehot.astype(jnp.float32)


def mlp_partial(
    whole, norm_gain_vector, gate_weight, up_weight, down_weight, adapter_table, onehot
):
    gate_up_input_maps, gate_up_output_maps, down_input_maps, down_output_maps = adapter_table
    rank_size = down_output_maps.shape[1]
    values = whole.astype(jnp.float32)
    mean_square = jnp.mean(values * values, axis=1, keepdims=True)
    normed_input = (
        values * lax.rsqrt(mean_square + EPSILON) * norm_gain_vector.astype(jnp.float32)
    ).astype(jnp.bfloat16)
    low_rank_term = jnp.einsum(
        "ec,mch->emh", normed_input, gate_up_input_maps, preferred_element_type=jnp.float32
    )
    low_rank_term = (low_rank_term * onehot[:, :, None]).astype(jnp.bfloat16)
    gate_sum = jnp.dot(normed_input, gate_weight, preferred_element_type=jnp.float32) + jnp.einsum(
        "vca,can->vn",
        low_rank_term[:, :, :rank_size],
        gate_up_output_maps[:, 0],
        preferred_element_type=jnp.float32,
    )
    up_sum = jnp.dot(normed_input, up_weight, preferred_element_type=jnp.float32) + jnp.einsum(
        "vca,can->vn",
        low_rank_term[:, :, rank_size:],
        gate_up_output_maps[:, 1],
        preferred_element_type=jnp.float32,
    )
    hidden = (jax.nn.silu(gate_sum) * up_sum).astype(jnp.bfloat16)
    down_rank = (
        jnp.einsum("tf,sfr->tsr", hidden, down_input_maps, preferred_element_type=jnp.float32)
        * onehot[:, :, None]
    )
    down_term = jnp.einsum(
        "tsr,srd->td",
        down_rank,
        down_output_maps.astype(jnp.float32),
        precision=lax.Precision.HIGHEST,
        preferred_element_type=jnp.float32,
    )
    return jnp.dot(hidden, down_weight, preferred_element_type=jnp.float32) + down_term


def on_device(
    tokens,
    norm_gain_vector,
    gate_weight,
    up_weight,
    down_weight,
    gate_up_input_maps,
    gate_up_output_maps,
    down_input_maps,
    down_output_maps,
    lengths,
    request_adapter_slot,
    selected,
):
    groups = lax.axis_size("req")
    device = lax.axis_index("req")
    capacity, columns = tokens.shape
    chosen_count = selected.shape[0]
    rank_size = down_output_maps.shape[1]
    width_size = down_output_maps.shape[2]
    inner_hidden = down_input_maps.shape[1]
    packed_adapters = gather_adapter_maps(
        gate_up_input_maps, gate_up_output_maps, down_input_maps, down_output_maps
    )
    every = lax.all_gather(packed_adapters, "req", axis=0, tiled=True)
    chosen = jnp.take(every, selected, axis=0)
    adapter_table = unpack_adapters(chosen, width_size, rank_size, inner_hidden)
    totals = jnp.sum(lengths, axis=1)
    block_rows = TOK_DEV // groups
    spread = capacity // TOK_DEV
    counts = totals // block_rows
    group_ends = jnp.cumsum(counts)
    offsets = group_ends - counts
    turn_by = offsets[device] % groups
    blocks = tokens.reshape(spread, groups, block_rows, columns)
    outgoing = jnp.roll(blocks, turn_by, axis=1)
    incoming = lax.all_to_all(outgoing, "req", split_axis=1, concat_axis=1, tiled=True)
    places = jnp.arange(groups, dtype=jnp.int32)
    global_ids = places * groups + device
    owners = jnp.sum((group_ends[None, :] <= global_ids[:, None]).astype(jnp.int32), axis=1)
    inner_ids = global_ids - jnp.take(offsets, owners)
    indices = inner_ids // groups * groups + owners
    flat_blocks = incoming.reshape(spread * groups, block_rows, columns)
    balanced = jnp.take(flat_blocks, indices, axis=0).reshape(groups * block_rows, columns)
    row_owner = jnp.repeat(owners, block_rows)
    row_position = (
        inner_ids[:, None] * block_rows + jnp.arange(block_rows, dtype=jnp.int32)[None, :]
    ).reshape(-1)
    onehot = slot_table(row_owner, row_position, lengths, request_adapter_slot, chosen_count)
    whole = lax.all_gather(balanced, "mlp", axis=1, tiled=True)
    partial_value = mlp_partial(
        whole, norm_gain_vector, gate_weight, up_weight, down_weight, adapter_table, onehot
    )
    branch = lax.psum_scatter(
        partial_value.astype(jnp.bfloat16), "mlp", scatter_dimension=1, tiled=True
    )
    back = (
        jnp.zeros((spread * groups, block_rows, columns), jnp.bfloat16)
        .at[indices]
        .set(branch.reshape(groups, block_rows, columns))
    )
    returned = lax.all_to_all(
        back.reshape(spread, groups, block_rows, columns),
        "req",
        split_axis=1,
        concat_axis=1,
        tiled=True,
    )
    branch_rows = jnp.roll(returned, -turn_by, axis=1).reshape(capacity, columns)
    branch_rows = lax.optimization_barrier(branch_rows).astype(jnp.float32)
    row_valid = jnp.arange(capacity, dtype=jnp.int32) < totals[device]
    values = tokens.astype(jnp.float32)
    return jnp.where(row_valid[:, None], values + branch_rows, values).astype(jnp.bfloat16)


def solution(mesh):
    in_specs = (
        P("req", "mlp"),
        P(),
        P(None, "mlp"),
        P(None, "mlp"),
        P("mlp", None),
        P("req", None, None),
        P("req", None, None, "mlp"),
        P("req", "mlp", None),
        P("req", None, None),
        P(),
        P(),
        P(),
    )
    out_specs = P("req", "mlp")
    return jax.shard_map(
        on_device, mesh=mesh, in_specs=in_specs, out_specs=out_specs, check_vma=False
    )
```

profile of v0, /device:TPU:0, one launch (start us, length us, event | category | flops | bytes accessed | tf_op | source)
XLA Modules:
  0.0 234.6 jit_solution(14905129458668095679)
XLA Ops:
  6.5 1.3 copy.45
  9.2 0.9 copy.62
  10.3 7.0 %maximum_bitcast_fusion = bf16[1,1,141312]{2,1,0:T(2,128)(2,1)} fusion(bf16[1,32768]{1,0:T(2,128)(2,1)S(1)} %bitcast.101, bf16[1,14336]{1,0:T(2,128)(2,1)S(1)} %reshape.320, bf16[1,28672]{1,0:T(2,128)(2,1)S(1)} %bitcast.104, bf16[1,65536]{1,0:T(2,128)(2,1)S(1)} %reshape.318), kind=kLoop, calls=%fused_computation.28 | loop fusion | flops 1130496 | bytes 565248
  20.6 1.0 copy.43
  21.6 7.3 %all-to-all-start = ((bf16[2,8,64,512]{3,2,0,1:T(8,128)(2,1)}), bf16[2,8,64,512]{3,2,0,1:T(8,128)(2,1)S(1)}, u32[]{:S(2)}, u32[]{:S(2)}) async-start(bf16[2,8,64,512]{3,2,0,1:T(8,128)(2,1)} %copy.43), calls=%async_computation | async-start | bytes 2097152 | tf_op jit(solution)/shard_map/all_to_all | solution.py:132
  30.4 1.0 gather_fusion.4
  31.9 1.0 gather_fusion.5
  33.5 39.2 %all-to-all-done = bf16[2,8,64,512]{3,2,0,1:T(8,128)(2,1)S(1)} async-done(((bf16[2,8,64,512]{3,2,0,1:T(8,128)(2,1)}), bf16[2,8,64,512]{3,2,0,1:T(8,128)(2,1)S(1)}, u32[]{:S(2)}, u32[]{:S(2)}) %all-to-all-start) | async-done | bytes 1048608 | tf_op jit(solution)/shard_map/all_to_all | solution.py:132
  73.4 1.0 bitcast_select_fusion
  74.7 43.2 %all-gather.6.cloned.1.call-done = bf16[8,1,141312]{2,1,0:T(2,128)(2,1)} async-done(((bf16[1,1,141312]{2,1,0:T(2,128)(2,1)}), bf16[8,1,141312]{2,1,0:T(2,128)(2,1)}) %all-gather.6.cloned.1.call-update) | async-done | bytes 2261008 | tf_op jit(solution)/shard_map/all_gather | solution.py:120
  117.9 3.4 %copy.70 = bf16[8,1,141312]{2,0,1:T(8,128)(2,1)S(1)} copy(bf16[8,1,141312]{2,1,0:T(2,128)(2,1)} %all-gather.6.cloned.1.call-done) | data formatting | bytes 4521984
  121.5 1.3 gather_fusion.2
  122.8 2.3 gather_fusion.3
  125.1 4.4 %maximum_select_fusion = bf16[8,141312]{1,0:T(8,128)(2,1)S(1)} fusion(bf16[8,70656]{1,0:T(8,128)(2,1)} %gather_fusion.3, bf16[8,70656]{1,0:T(8,128)(2,1)S(1)} %gather_fusion.2, pred[8]{0:T(512)(128)(4,1)S(1)} %get-tuple-element.13), kind=kLoop, calls=%fused_computation.15 | loop fusion | flops 5652480 | bytes 4521992 | tf_op jit(solution)/shard_map/jit(_take)/select_n | solution.py:121
  129.6 1.3 copy-done
  130.9 5.0 %reshape.322 = bf16[8,2048,32]{2,1,0:T(8,128)(2,1)} reshape(bf16[8,65536]{1,0:T(8,128)(2,1)S(1)} %slice.44) | data formatting | bytes 2097152 | tf_op jit(solution)/shard_map/reshape | solution.py:30
  135.9 4.6 %copy.47 = bf16[8,2048,32]{1,2,0:T(8,128)(2,1)} copy(bf16[8,2048,32]{2,1,0:T(8,128)(2,1)} %reshape.322) | data formatting | bytes 2097152 | tf_op jit(solution)/shard_map/reshape | solution.py:30
  140.6 1.5 reshape.325
  142.1 0.9 copy.52
  143.1 2.2 fusion
  145.4 2.1 fusion.27
  147.9 1.6 copy-done.9
  149.5 2.4 %fusion.29 = f32[512,896]{1,0:T(8,128)S(1)} fusion(bf16[2048,896]{1,0:T(8,128)(2,1)S(1)} %copy-done.9, bf16[512,2048]{1,0:T(8,128)(2,1)S(1)} %copy-done.3, f32[2048]{0:T(1024)S(1)} %convert_element_type.41, f32[512]{0:T(512)S(1)} %add_rsqrt_fusion), kind=kOutput, calls=%fused_computation.94 | convolution fusion | flops 1883242496 | bytes 7612416 | tf_op jit(solution)/shard_map/dot_general | solution.py:69
  151.9 2.4 %fusion.25 = f32[512,896]{1,0:T(8,128)S(1)} fusion(bf16[2048,896]{1,0:T(8,128)(2,1)S(1)} %copy-done.10, bf16[512,2048]{1,0:T(8,128)(2,1)S(1)} %copy-done.3, f32[2048]{0:T(1024)S(1)} %convert_element_type.41, f32[512]{0:T(512)S(1)} %add_rsqrt_fusion), kind=kOutput, calls=%fused_computation.92 | convolution fusion | flops 1883242496 | bytes 7612416 | tf_op jit(solution)/shard_map/dot_general | solution.py:75
  156.4 2.3 fusion.35
  158.7 3.5 %fusion.3 = bf16[512,2048]{1,0:T(8,128)(2,1)} fusion(f32[512,2048]{1,0:T(8,128)S(1)} %fusion.35, bf16[1,8,16,2048]{3,1,2,0:T(8,128)(2,1)S(1)} %bitcast.93, f32[512,8,16]{0,2,1:T(8,128)S(1)} %bitcast.107, f32[512,8]{0,1:T(8,128)S(1)} %fusion.19), kind=kOutput, calls=%fused_computation.13 | convolution fusion | flops 1612775424 | bytes 7094272 | tf_op jit(solution)/shard_map/tsr,srd->td/dot_general | solution.py:86
  162.2 29.7 %reduce-scatter.2.cloned.1.call-done = bf16[512,512]{1,0:T(8,128)(2,1)} async-done(((bf16[512,2048]{1,0:T(8,128)(2,1)}), bf16[512,512]{1,0:T(8,128)(2,1)}) %reduce-scatter.2.cloned.1.call-update) | async-done | bytes 524304 | tf_op jit(solution)/shard_map/reduce_scatter | solution.py:149
  192.0 1.8 scatter_fusion
  193.8 1.1 copy.53
  194.9 5.5 %all-to-all-start.1 = ((bf16[2,8,64,512]{3,2,0,1:T(8,128)(2,1)}), bf16[2,8,64,512]{3,2,0,1:T(8,128)(2,1)S(1)}, u32[]{:S(2)}, u32[]{:S(2)}) async-start(bf16[2,8,64,512]{3,2,0,1:T(8,128)(2,1)} %copy.53), calls=%async_computation.2 | async-start | bytes 2097152 | tf_op jit(solution)/shard_map/all_to_all | solution.py:157
  201.7 24.5 %all-to-all-done.1 = bf16[2,8,64,512]{3,2,0,1:T(8,128)(2,1)S(1)} async-done(((bf16[2,8,64,512]{3,2,0,1:T(8,128)(2,1)}), bf16[2,8,64,512]{3,2,0,1:T(8,128)(2,1)S(1)}, u32[]{:S(2)}, u32[]{:S(2)}) %all-to-all-start.1) | async-done | bytes 1048608 | tf_op jit(solution)/shard_map/all_to_all | solution.py:157
  226.6 1.4 fusion.4
  (88 shorter events, 10.8 us)
Async XLA Ops:
  6.5 3.7 %copy-start.4 = (bf16[1,2,16,896]{3,2,1,0:T(8,128)(2,1)S(1)}, bf16[1,2,16,896]{3,2,1,0:T(8,128)(2,1)}, u32[]{:S(2)}) copy-start(bf16[1,2,16,896]{3,2,1,0:T(8,128)(2,1)} %param.22) | copy-start | bytes 172036
  6.5 10.8 %copy-start.5 = (s32[8,4]{0,1:T(4,128)S(1)}, s32[8,4]{0,1:T(4,128)}, u32[]{:S(2)}) copy-start(s32[8,4]{0,1:T(4,128)} %param.25) | copy-start | bytes 388
  6.5 13.6 %copy-start.1 = (bf16[1024,512]{1,0:T(8,128)(2,1)S(1)}, bf16[1024,512]{1,0:T(8,128)(2,1)}, u32[]{:S(2)}) copy-start(bf16[1024,512]{1,0:T(8,128)(2,1)} %param.16) | copy-start | bytes 3145732
  6.5 111.3 %all-gather.6.cloned.1.call-start = ((), (), s32[]{:S(2)}) async-start(), calls=%async_computation.5 | async-start | bytes 5087232 | tf_op jit(solution)/shard_map/all_gather | solution.py:120
  20.5 9.3 %copy-start.8 = (s32[8]{0:T(128)S(1)}, s32[8]{0:T(128)}, u32[]{:S(2)}) copy-start(s32[8]{0:T(128)} %param.27) | copy-start | bytes 100
  20.5 9.5 %copy-start.6 = (bf16[2048]{0:T(1024)(128)(2,1)S(1)}, bf16[2048]{0:T(1024)(128)(2,1)}, u32[]{:S(2)}) copy-start(bf16[2048]{0:T(1024)(128)(2,1)} %param.17) | copy-start | bytes 12292
  21.6 51.1 %all-to-all-start = ((bf16[2,8,64,512]{3,2,0,1:T(8,128)(2,1)}), bf16[2,8,64,512]{3,2,0,1:T(8,128)(2,1)S(1)}, u32[]{:S(2)}, u32[]{:S(2)}) async-start(bf16[2,8,64,512]{3,2,0,1:T(8,128)(2,1)} %copy.43), calls=%async_computation | async-start | bytes 2097152 | tf_op jit(solution)/shard_map/all_to_all | solution.py:132
  28.8 2.9 %copy-start.7 = (s32[8,4]{0,1:T(4,128)S(1)}, s32[8,4]{0,1:T(4,128)}, u32[]{:S(2)}) copy-start(s32[8,4]{0,1:T(4,128)} %param.26) | copy-start | bytes 388
  28.8 114.3 %all-gather.4.cloned.1.call-start = ((), (), s32[]{:S(2)}) async-start(), calls=%async_computation.3 | async-start | bytes 2621440 | tf_op jit(solution)/shard_map/all_gather | solution.py:145
  74.4 117.5 %reduce-scatter.2.cloned.1.call-start = ((), (), s32[]{:S(2)}) async-start(), calls=%async_computation.4 | async-start | bytes 2621440 | tf_op jit(solution)/shard_map/reduce_scatter | solution.py:149
  129.5 1.4 copy-start
  135.9 4.6 %slice-start = ((bf16[8,141312]{1,0:T(8,128)(2,1)}), bf16[8,28672]{1,0:T(8,128)(2,1)S(1)}, s32[]{:S(2)}) async-start(bf16[8,141312]{1,0:T(8,128)(2,1)} %copy-done), calls=%async_computation.6 | async-start | bytes 917504 | tf_op jit(solution)/shard_map/slice | solution.py:33
  135.9 4.7 %slice-start.1 = ((bf16[8,141312]{1,0:T(8,128)(2,1)}), bf16[8,14336]{1,0:T(8,128)(2,1)S(1)}, s32[]{:S(2)}) async-start(bf16[8,141312]{1,0:T(8,128)(2,1)} %copy-done), calls=%async_computation.7 | async-start | bytes 458752 | tf_op jit(solution)/shard_map/slice | solution.py:36
  143.1 2.2 copy-start.3
  147.5 2.0 copy-start.9
  149.5 2.4 %copy-start.10 = (bf16[2048,896]{1,0:T(8,128)(2,1)S(1)}, bf16[2048,896]{1,0:T(8,128)(2,1)}, u32[]{:S(2)}) copy-start(bf16[2048,896]{1,0:T(8,128)(2,1)} %param.19) | copy-start | bytes 11010052
  154.3 2.0 copy-start.11
  156.4 2.3 slice-start.2
  194.9 31.3 %all-to-all-start.1 = ((bf16[2,8,64,512]{3,2,0,1:T(8,128)(2,1)}), bf16[2,8,64,512]{3,2,0,1:T(8,128)(2,1)S(1)}, u32[]{:S(2)}, u32[]{:S(2)}) async-start(bf16[2,8,64,512]{3,2,0,1:T(8,128)(2,1)} %copy.53), calls=%async_computation.2 | async-start | bytes 2097152 | tf_op jit(solution)/shard_map/all_to_all | solution.py:157
  201.7 25.0 %copy-start.2 = (bf16[1024,512]{1,0:T(8,128)(2,1)S(1)}, bf16[1024,512]{1,0:T(8,128)(2,1)}, u32[]{:S(2)}) copy-start(bf16[1024,512]{1,0:T(8,128)(2,1)} %param.16) | copy-start | bytes 3145732
Sparse Core Ops, SparseCore 0:
  17.4 100.3 all-gather.5
  119.4 20.7 all-gather.3
  162.3 29.5 reduce-scatter.1
where the time goes:
time: 235 us
  waiting for transfers between devices  137 us (58%)
  local copies, waits for them, and re-layouts  36.1 us (15%)
  other arithmetic  19 us (8%)
  between operations  15.5 us (7%)
  matrix products  14.3 us (6%)
  starting transfers between devices  13.1 us (6%)
    all_gather x1, waiting for transfers between devices, on_device(): every = lax.all_gather(packed_adapters, 'req', axis=0, tiled=True)  43.2 us
    all_to_all x1, waiting for transfers between devices, on_device(): lax.all_to_all(outgoing, 'req', split_axis=1, concat_axis=1, tiled=True)  39.2 us
    reduce_scatter x1, waiting for transfers between devices, on_device(): lax.psum_scatter(partial_value.astype(jnp.bfloat16), 'mlp', scatter_dimen...  29.7 us
    all_to_all x1, waiting for transfers between devices, on_device(): lax.all_to_all(back.reshape(spread, groups, block_rows, columns), 'req',...  24.5 us
    unnamed x33, local copies, waits for them, and re-layouts  10.7 us
    reshape x2, local copies, waits for them, and re-layouts, unpack_adapters(): packed_adapters[:, :first_branch]  9.65 us
    all_to_all x1, starting transfers between devices, on_device(): lax.all_to_all(outgoing, 'req', split_axis=1, concat_axis=1, tiled=True)  7.25 us
    unnamed x1, other arithmetic  6.99 us
  transfers between devices with their start and end apart: 5, of which 4 were waited for; matrix products, arithmetic and copies ran while one was open for 14% of the time, Pallas kernels for 0%

commit v1 on v0

v1 whole, which is shorter than its diff:
```python
import functools

import jax
import jax.numpy as jnp
from jax import lax
from jax.experimental import pallas as pl
from jax.experimental.pallas import tpu as pltpu
from jax.sharding import PartitionSpec as P

EPSILON = 1e-06
CHUNKS = 4
MESH = pl.DeviceIdType.MESH
NT = (((1,), (1,)), ((), ()))


def kernel(
    groups,
    owned,
    rank,
    slots,
    ids_ref,
    total_ref,
    tokens_ref,
    gain_ref,
    gate_ref,
    up_ref,
    down_ref,
    pack_ref,
    low_ref,
    high_ref,
    out_ref,
    gate_v,
    up_v,
    down_v,
    whole,
    normed,
    hidden,
    maps,
    maps_sib,
    a_sel,
    bg_sel,
    bu_sel,
    da_sel,
    db_sel,
    own_part,
    sib_out,
    sib_in,
    far_out,
    far_in,
    ad_s,
    ad_r,
    af_s,
    af_r,
    ts_s,
    ts_r,
    tc_s,
    tc_r,
    tf_s,
    tf_r,
    rs_s,
    rs_r,
    rc_s,
    rc_r,
    local_sem,
):
    r = lax.axis_index("req")
    m = lax.axis_index("mlp")
    half = lax.rem(m, 2)
    sib = m + 1 - 2 * half
    side = m // 2
    far = m + 2 - 4 * side
    diag = sib + 2 - 4 * side
    rows, cols = tokens_ref.shape
    rc = rows // CHUNKS
    hwidth = maps_sib.shape[2]
    inner = gate_v.shape[1]
    prow = pack_ref.shape[0]

    def local(i, src, dst):
        return pltpu.make_async_copy(src, dst, local_sem.at[i])

    def remote(src, dst, ss, rs, axis, dev):
        return pltpu.make_async_remote_copy(
            src_ref=src,
            dst_ref=dst,
            send_sem=ss,
            recv_sem=rs,
            device_id={axis: dev},
            device_id_type=MESH,
        )

    def rows_of(k):
        return pl.ds(pl.multiple_of(k * rc, rc), rc)

    def slot_of(g):
        return maps.at[g]

    def ad_copy(i):
        return remote(
            pack_ref, slot_of(r), ad_s.at[i], ad_r.at[i], "req", lax.rem(r + i, groups)
        )

    def ad_wait(i):
        src = lax.rem(r + groups - i, groups)
        return remote(pack_ref, slot_of(src), ad_s.at[i], ad_r.at[i], "req", src)

    def af_copy(i):
        src = lax.rem(r + groups - i, groups)
        return remote(
            maps.at[src, :, pl.ds(0, hwidth)],
            maps_sib.at[src],
            af_s.at[i],
            af_r.at[i],
            "mlp",
            sib,
        )

    def tok_sib(k, who):
        return remote(
            tokens_ref.at[rows_of(k)], whole.at[who, rows_of(k)], ts_s.at[k], ts_r.at[k], "mlp", sib
        )

    def tok_far(k, who):
        return remote(
            tokens_ref.at[rows_of(k)], whole.at[who, rows_of(k)], tc_s.at[k], tc_r.at[k], "mlp", far
        )

    def tok_fwd(k, who):
        return remote(
            whole.at[far, rows_of(k)], whole.at[who, rows_of(k)], tf_s.at[k], tf_r.at[k], "mlp", sib
        )

    def part_sib(k):
        return remote(sib_out.at[k], sib_in.at[k], rs_s.at[k], rs_r.at[k], "mlp", sib)

    def part_far(k):
        return remote(far_out.at[k], far_in.at[k], rc_s.at[k], rc_r.at[k], "mlp", far)

    w_copies = [
        local(0, gate_ref, gate_v),
        local(1, up_ref, up_v),
        local(2, down_ref, down_v),
        local(3, tokens_ref, whole.at[m]),
        local(4, pack_ref, slot_of(r)),
    ]

    barrier = pltpu.get_barrier_semaphore()

    def greet(i, carry):
        pl.semaphore_signal(
            barrier, inc=1, device_id={"req": lax.rem(r + i, groups)}, device_id_type=MESH
        )
        return carry

    lax.fori_loop(1, groups, greet, 0)
    pl.semaphore_signal(barrier, inc=1, device_id={"mlp": sib}, device_id_type=MESH)
    pl.semaphore_signal(barrier, inc=1, device_id={"mlp": far}, device_id_type=MESH)
    pl.semaphore_wait(barrier, groups + 1)

    def each(n, start=0):
        def deco(f):
            def body(i, carry):
                f(i)
                return carry

            lax.fori_loop(start, n, body, 0)

        return deco

    @each(CHUNKS)
    def _(k):
        tok_far(k, m).start()
        tok_sib(k, m).start()

    @each(groups, 1)
    def _(i):
        ad_copy(i).start()

    for j in (4, 3, 0, 1, 2):
        w_copies[j].start()
    w_copies[4].wait()
    w_copies[3].wait()
    af_copy(0).start()

    def pass_on(k):
        tok_far(k, far).wait_recv()
        tok_fwd(k, far).start()

    pass_on(0)

    @each(groups, 1)
    def _(i):
        ad_wait(i).wait_recv()
        af_copy(i).start()

    @each(groups)
    def _(i):
        af_copy(i).wait_recv()

    span = slots * rank
    bg_sel[...] = jnp.zeros_like(bg_sel)
    bu_sel[...] = jnp.zeros_like(bu_sel)
    mine = pl.ds(pl.multiple_of(half * hwidth, hwidth), hwidth)
    other = pl.ds(pl.multiple_of((1 - half) * hwidth, hwidth), hwidth)
    per = prow // owned
    for q in range(slots):
        g = ids_ref[0, q]
        at = pl.ds(q * rank, rank)
        at2 = pl.ds(span + q * rank, rank)
        row0 = ids_ref[1, q] * per if owned > 1 else 0
        for dst, part in ((mine, maps), (other, maps_sib)):
            a_sel[at, dst] = part[g, pl.ds(row0, rank), 0:hwidth]
            a_sel[at2, dst] = part[g, pl.ds(row0 + rank, rank), 0:hwidth]
            db = part[g, pl.ds(row0 + 2 * rank, rank), 0:hwidth]
            db_sel[at, dst] = db
            db_sel[at2, dst] = db
        bg_sel[at, :] = maps[g, pl.ds(row0, rank), hwidth : hwidth + inner]
        bu_sel[at2, :] = maps[g, pl.ds(row0 + rank, rank), hwidth : hwidth + inner]
        da = maps[g, pl.ds(row0 + 2 * rank, rank), hwidth : hwidth + inner]
        da_sel[at, :] = da
        da_sel[at2, :] = da
    for j in (0, 1, 2):
        w_copies[j].wait()

    parts = whole.shape[0]
    f32 = jnp.float32

    def reduce_far(k):
        part_sib(k).wait_recv()
        far_out[k] = (own_part[k, 0] + sib_in[k, 0].astype(f32)).astype(jnp.bfloat16)
        part_far(k).start()

    @each(CHUNKS)
    def _(k):
        here = rows_of(k)

        @pl.when(k < CHUNKS - 1)
        def _():
            pass_on(k + 1)

        tok_sib(k, sib).wait_recv()
        tok_fwd(k, diag).wait_recv()
        squares = jnp.zeros((rc, 1), f32)
        for b in range(parts):
            x = whole[b, here, :].astype(f32)
            squares += jnp.sum(x * x, axis=1, keepdims=True)
        scale = lax.rsqrt(squares / (parts * cols) + EPSILON)
        for b in range(parts):
            x = whole[b, here, :].astype(f32)
            gain = gain_ref[:, b * cols : (b + 1) * cols].astype(f32)
            normed[:, b * cols : (b + 1) * cols] = (x * scale * gain).astype(jnp.bfloat16)
        at = lax.broadcasted_iota(jnp.int32, (rc, 2 * span), 0) + k * rc
        live = (at >= low_ref[...]) & (at < high_ref[...])
        low_rank = lax.dot_general(normed[...], a_sel[...], NT, preferred_element_type=f32)
        low_rank = jnp.where(live, low_rank, 0.0).astype(jnp.bfloat16)
        for n0 in range(0, inner, 256):
            n1 = min(n0 + 256, inner)
            g = jnp.dot(normed[...], gate_v[:, n0:n1], preferred_element_type=f32)
            g += jnp.dot(low_rank, bg_sel[:, n0:n1], preferred_element_type=f32)
            u = jnp.dot(normed[...], up_v[:, n0:n1], preferred_element_type=f32)
            u += jnp.dot(low_rank, bu_sel[:, n0:n1], preferred_element_type=f32)
            hidden[:, n0:n1] = (jax.nn.silu(g) * u).astype(jnp.bfloat16)
        down_rank = lax.dot_general(hidden[...], da_sel[...], NT, preferred_element_type=f32)
        down_rank = jnp.where(live, down_rank, 0.0)
        coarse = down_rank.astype(jnp.bfloat16).astype(f32)
        lane = lax.broadcasted_iota(jnp.int32, (rc, 2 * span), 1)
        down_rank = jnp.where(lane < span, coarse, down_rank - coarse).astype(jnp.bfloat16)

        def part_of(b):
            there = pl.ds(pl.multiple_of(b * cols, cols), cols)
            return jnp.dot(hidden[...], down_v[:, there], preferred_element_type=f32) + jnp.dot(
                down_rank, db_sel[:, there], preferred_element_type=f32
            )

        sib_out[k, 0] = part_of(diag).astype(jnp.bfloat16)
        sib_out[k, 1] = part_of(sib).astype(jnp.bfloat16)
        part_sib(k).start()
        own_part[k, 0] = part_of(far)

        @pl.when(k > 0)
        def _():
            reduce_far(k - 1)

        own_part[k, 1] = part_of(m)

    reduce_far(CHUNKS - 1)
    total = total_ref[0]

    @each(CHUNKS)
    def _(k):
        here = rows_of(k)
        part_far(k).wait_recv()
        branch = own_part[k, 1] + sib_in[k, 1].astype(f32) + far_in[k].astype(f32)
        branch = branch.astype(jnp.bfloat16).astype(f32)
        at = lax.broadcasted_iota(jnp.int32, (rc, cols), 0) + k * rc
        x = whole[m, here, :].astype(f32)
        out_ref[here, :] = jnp.where(at < total, x + branch, x).astype(out_ref.dtype)

    @each(CHUNKS)
    def _(k):
        tok_far(k, m).wait_send()
        tok_sib(k, m).wait_send()
        tok_fwd(k, far).wait_send()
        part_sib(k).wait_send()
        part_far(k).wait_send()

    @each(groups, 1)
    def _(i):
        ad_copy(i).wait_send()

    @each(groups)
    def _(i):
        af_copy(i).wait_send()


def on_device(
    tokens,
    norm_gain_vector,
    gate_weight,
    up_weight,
    down_weight,
    gate_up_input_maps,
    gate_up_output_maps,
    down_input_maps,
    down_output_maps,
    lengths,
    request_adapter_slot,
    selected,
):
    groups = lax.axis_size("req")
    r = lax.axis_index("req")
    m = lax.axis_index("mlp")
    parts = lax.axis_size("mlp")
    rows, cols = tokens.shape
    owned, rank, width = down_output_maps.shape
    inner = gate_weight.shape[1]
    slots = lengths.shape[1]
    span = slots * rank
    hwidth = width // 2
    bf16 = jnp.bfloat16

    shared = jnp.concatenate(
        [jnp.swapaxes(gate_up_input_maps, 1, 2), down_output_maps], axis=1
    )
    shared = lax.dynamic_slice_in_dim(shared, (m % 2) * hwidth, hwidth, axis=2)
    own = jnp.concatenate(
        [
            gate_up_output_maps.reshape(owned, 2 * rank, inner),
            jnp.swapaxes(down_input_maps, 1, 2),
        ],
        axis=1,
    )
    pack = jnp.concatenate([shared, own], axis=2).reshape(owned * 3 * rank, hwidth + inner)

    lens = lengths[r]
    ends = jnp.cumsum(lens)
    starts = ends - lens
    ids = selected[request_adapter_slot[r]]
    ids = jnp.stack([ids // owned, ids % owned]).astype(jnp.int32)
    low = jnp.tile(jnp.repeat(starts, rank), 2).reshape(1, 2 * span)
    high = jnp.tile(jnp.repeat(ends, rank), 2).reshape(1, 2 * span)
    total = ends[slots - 1 :]

    rc = rows // CHUNKS
    vm, sm, hbm = (
        pl.BlockSpec(memory_space=s) for s in (pltpu.VMEM, pltpu.SMEM, pl.ANY)
    )
    dma = pltpu.SemaphoreType.DMA
    return pl.pallas_call(
        functools.partial(kernel, groups, owned, rank, slots),
        out_shape=jax.ShapeDtypeStruct((rows, cols), tokens.dtype),
        in_specs=[sm, sm, hbm, vm, hbm, hbm, hbm, hbm, vm, vm],
        out_specs=vm,
        scratch_shapes=[
            pltpu.VMEM((width, inner), bf16),
            pltpu.VMEM((width, inner), bf16),
            pltpu.VMEM((inner, width), bf16),
            pltpu.VMEM((parts, rows, cols), bf16),
            pltpu.VMEM((rc, width), bf16),
            pltpu.VMEM((rc, inner), bf16),
            pltpu.VMEM((groups,) + pack.shape, bf16),
            pltpu.VMEM((groups, pack.shape[0], hwidth), bf16),
            pltpu.VMEM((2 * span, width), bf16),
            pltpu.VMEM((2 * span, inner), bf16),
            pltpu.VMEM((2 * span, inner), bf16),
            pltpu.VMEM((2 * span, inner), bf16),
            pltpu.VMEM((2 * span, width), bf16),
            pltpu.VMEM((CHUNKS, 2, rc, cols), jnp.float32),
            pltpu.VMEM((CHUNKS, 2, rc, cols), bf16),
            pltpu.VMEM((CHUNKS, 2, rc, cols), bf16),
            pltpu.VMEM((CHUNKS, rc, cols), bf16),
            pltpu.VMEM((CHUNKS, rc, cols), bf16),
            dma((groups,)),
            dma((groups,)),
            dma((groups,)),
            dma((groups,)),
        ]
        + [dma((CHUNKS,)) for _ in range(10)]
        + [dma((5,))],
        compiler_params=pltpu.CompilerParams(
            collective_id=0, has_side_effects=True, vmem_limit_bytes=60 * 1024 * 1024
        ),
    )(
        ids,
        total,
        tokens,
        norm_gain_vector.reshape(1, width),
        gate_weight,
        up_weight,
        down_weight,
        pack,
        low,
        high,
    )


def solution(mesh):
    in_specs = (
        P("req", "mlp"),
        P(),
        P(None, "mlp"),
        P(None, "mlp"),
        P("mlp", None),
        P("req", None, None),
        P("req", None, None, "mlp"),
        P("req", "mlp", None),
        P("req", None, None),
        P(),
        P(),
        P(),
    )
    return jax.shard_map(
        on_device, mesh=mesh, in_specs=in_specs, out_specs=P("req", "mlp"), check_vma=False
    )
```

time: 235 us -> 89.9 us (0.38)
  the two profiles are of different devices: /device:TPU:0 before, /device:TPU:11 now
where the time goes in v1:
time: 89.9 us; the launch traced here: 89.6 us
  Pallas kernels  79.1 us (88%)
  local copies, waits for them, and re-layouts  7.87 us (9%)
  other arithmetic  2.57 us (3%)
    pallas_call x1, Pallas kernels, on_device(): pl.pallas_call(functools.partial(kernel, groups, owned, rank, slots), out...  79.1 us
    unnamed x3, local copies, waits for them, and re-layouts  2.27 us

profile of v1, /device:TPU:11, one launch (start us, length us, event | category | flops | bytes accessed | tf_op | source)
XLA Modules:
  0.0 89.6 jit_solution(13172208321549862784)
XLA Ops:
  0.0 0.0 copy-start
  0.0 0.9 %dynamic-slice_reduce_fusion = (s32[4]{0:T(128)S(1)}, s32[4]{0:T(128)S(1)}) fusion(s32[8,4]{0,1:T(4,128)} %param.21, s32[]{:T(128)S(6)} %select_n.36, s32[8,4]{0,1:T(4,128)} %param.22), kind=kLoop, calls=%fused_computation.7 | loop fusion | bytes 68 | tf_op jit(solution)/shard_map/dynamic_slice | solution.py:355
  0.9 0.2 reduce-window.4
  1.1 0.6 slice.6
  1.7 0.1 broadcast_in_dim.8
  1.8 0.1 tile.16
  1.9 0.6 reshape_tile.7.high_ref
  2.5 0.1 broadcast_in_dim.7
  2.5 0.1 tile.14
  2.6 0.7 reshape_tile.6.low_ref
  3.3 0.0 copy-done
  3.3 0.6 gather_fusion
  3.9 0.6 stack.2.ids_ref
  4.5 1.3 %reshape.51.gain_ref = bf16[1,2048]{1,0:T(2,128)(2,1)} reshape(bf16[2048]{0:T(1024)(128)(2,1)} %param.13) | data formatting | bytes 8192 | tf_op jit(solution)/shard_map/reshape | solution.py:407
  5.8 0.8 fusion
  6.7 1.5 %maximum_bitcast_fusion.pack_ref = bf16[48,1920]{1,0:T(8,128)(2,1)} fusion(bf16[1,16,896]{2,1,0:T(8,128)(2,1)} %bitcast.16, bf16[1,32,896]{2,1,0:T(8,128)(2,1)} %bitcast.15, bf16[1,48,1024]{2,1,0:T(8,128)(2,1)S(1)} %fusion), kind=kLoop, calls=%fused_computation.3 | loop fusion | flops 552960 | bytes 368640 | tf_op jit(solution)/shard_map/reshape | solution.py:353
  8.2 79.1 %shard_map.118 = bf16[1024,512]{1,0:T(8,128)(2,1)} custom-call(s32[2,4]{1,0:T(2,128)} %stack.2.ids_ref, s32[1]{0:T(128)} %bitcast.2.total_ref, bf16[1024,512]{1,0:T(8,128)(2,1)} %tokens_ref.1, bf16[1,2048]{1,0:T(2,128)(2,1)} %reshape.51.gain_ref, bf16[2048,896]{1,0:T(8,128)(2,1)} %gate_ref.1, bf16[2048,896]{1,0:T(8,128)(2,1)} %up_ref.1, ...), custom_call_target="tpu_custom_call" | custom-call | tf_op jit(solution)/shard_map/pallas_call | solution.py:369
  87.3 2.3 %copy.14 = bf16[1024,512]{1,0:T(8,128)(2,1)} copy(bf16[1024,512]{1,0:T(8,128)(2,1)} %shard_map.118) | data formatting | bytes 2097152
  (5 shorter events, 0.0 us)
Async XLA Ops:
  0.0 3.3 %copy-start = (s32[8]{0:T(128)S(1)}, s32[8]{0:T(128)}, u32[]{:S(2)}) copy-start(s32[8]{0:T(128)} %param.23) | copy-start | bytes 100

commit v2 on v1

--- a/solution.py
+++ b/solution.py
@@ -18,16 +18,18 @@
     owned,
     rank,
     slots,
-    ids_ref,
-    total_ref,
+    lengths_ref,
+    slot_ref,
+    chosen_ref,
     tokens_ref,
     gain_ref,
     gate_ref,
     up_ref,
     down_ref,
-    pack_ref,
-    low_ref,
-    high_ref,
+    a_ref,
+    b_ref,
+    da_ref,
+    db_ref,
     out_ref,
     gate_v,
     up_v,
@@ -47,8 +49,11 @@
     sib_in,
     far_out,
     far_in,
-    ad_s,
-    ad_r,
+    up_s,
+    dn_s,
+    line_r,
+    cross_s,
+    cross_r,
     af_s,
     af_r,
     ts_s,
@@ -70,11 +75,15 @@
     side = m // 2
     far = m + 2 - 4 * side
     diag = sib + 2 - 4 * side
+    lane = lax.rem(r, 2)
+    partner = r + 1 - 2 * lane
+    place = r // 2
+    places = groups // 2
     rows, cols = tokens_ref.shape
     rc = rows // CHUNKS
     hwidth = maps_sib.shape[2]
     inner = gate_v.shape[1]
-    prow = pack_ref.shape[0]
+    span = slots * rank
 
     def local(i, src, dst):
         return pltpu.make_async_copy(src, dst, local_sem.at[i])
@@ -92,27 +101,21 @@
     def rows_of(k):
         return pl.ds(pl.multiple_of(k * rc, rc), rc)
 
-    def slot_of(g):
-        return maps.at[g]
-
-    def ad_copy(i):
+    def up_copy(i):
+        slot = maps.at[2 * i + lane]
+        return remote(slot, slot, up_s.at[i], line_r.at[i], "req", r + 2)
+
+    def down_copy(i):
+        slot = maps.at[2 * i + lane]
+        return remote(slot, slot, dn_s.at[i], line_r.at[i], "req", r - 2)
+
+    def cross_copy(i, side_of):
+        slot = maps.at[2 * i + side_of]
+        return remote(slot, slot, cross_s.at[i], cross_r.at[i], "req", partner)
+
+    def af_copy(g):
         return remote(
-            pack_ref, slot_of(r), ad_s.at[i], ad_r.at[i], "req", lax.rem(r + i, groups)
-        )
-
-    def ad_wait(i):
-        src = lax.rem(r + groups - i, groups)
-        return remote(pack_ref, slot_of(src), ad_s.at[i], ad_r.at[i], "req", src)
-
-    def af_copy(i):
-        src = lax.rem(r + groups - i, groups)
-        return remote(
-            maps.at[src, :, pl.ds(0, hwidth)],
-            maps_sib.at[src],
-            af_s.at[i],
-            af_r.at[i],
-            "mlp",
-            sib,
+            maps.at[g, :, pl.ds(0, hwidth)], maps_sib.at[g], af_s.at[g], af_r.at[g], "mlp", sib
         )
 
     def tok_sib(k, who):
@@ -141,21 +144,46 @@
         local(1, up_ref, up_v),
         local(2, down_ref, down_v),
         local(3, tokens_ref, whole.at[m]),
-        local(4, pack_ref, slot_of(r)),
     ]
+    mine = pl.ds(pl.multiple_of(half * hwidth, hwidth), hwidth)
+    other = pl.ds(pl.multiple_of((1 - half) * hwidth, hwidth), hwidth)
+    per = 3 * rank
+    packs = []
+    for o in range(owned):
+        first, last = pl.ds(o * per, 2 * rank), pl.ds(o * per + 2 * rank, rank)
+        left, right = pl.ds(0, hwidth), pl.ds(hwidth, inner)
+        packs += [
+            (a_ref.at[o, :, mine], maps.at[r, first, left]),
+            (b_ref.at[o], maps.at[r, first, right]),
+            (da_ref.at[o], maps.at[r, last, right]),
+            (db_ref.at[o, :, mine], maps.at[r, last, left]),
+        ]
+    packs = [local(4 + i, src, dst) for i, (src, dst) in enumerate(packs)]
+    for copy in packs:
+        copy.start()
 
     barrier = pltpu.get_barrier_semaphore()
 
-    def greet(i, carry):
-        pl.semaphore_signal(
-            barrier, inc=1, device_id={"req": lax.rem(r + i, groups)}, device_id_type=MESH
-        )
-        return carry
-
-    lax.fori_loop(1, groups, greet, 0)
-    pl.semaphore_signal(barrier, inc=1, device_id={"mlp": sib}, device_id_type=MESH)
-    pl.semaphore_signal(barrier, inc=1, device_id={"mlp": far}, device_id_type=MESH)
-    pl.semaphore_wait(barrier, groups + 1)
+    def greet(axis, dev):
+        pl.semaphore_signal(barrier, inc=1, device_id={axis: dev}, device_id_type=MESH)
+
+    greet("mlp", sib)
+    greet("mlp", far)
+    greet("req", partner)
+    inner_up = place < places - 1
+    inner_down = place > 0
+
+    @pl.when(inner_up)
+    def _():
+        greet("req", r + 2)
+
+    @pl.when(inner_down)
+    def _():
+        greet("req", r - 2)
+
+    below = (place + places - 1) // places
+    above = (2 * (places - 1) - place) // places
+    pl.semaphore_wait(barrier, 3 + below + above)
 
     def each(n, start=0):
         def deco(f):
@@ -172,42 +200,80 @@
         tok_far(k, m).start()
         tok_sib(k, m).start()
 
-    @each(groups, 1)
-    def _(i):
-        ad_copy(i).start()
-
-    for j in (4, 3, 0, 1, 2):
-        w_copies[j].start()
-    w_copies[4].wait()
-    w_copies[3].wait()
-    af_copy(0).start()
-
     def pass_on(k):
         tok_far(k, far).wait_recv()
         tok_fwd(k, far).start()
 
+    for copy in packs:
+        copy.wait()
+
+    @pl.when(inner_up)
+    def _():
+        up_copy(place).start()
+
+    @pl.when(inner_down)
+    def _():
+        down_copy(place).start()
+
+    cross_copy(place, lane).start()
+    af_copy(r).start()
+
+    for j in (3, 0, 1, 2):
+        w_copies[j].start()
     pass_on(0)
 
-    @each(groups, 1)
+    @each(places, 1)
+    def _(d):
+        @pl.when(place - d >= 0)
+        def _():
+            i = place - d
+            up_copy(i).wait_recv()
+
+            @pl.when(inner_up)
+            def _():
+                up_copy(i).start()
+
+            cross_copy(i, lane).start()
+            af_copy(2 * i + lane).start()
+
+        @pl.when(place + d < places)
+        def _():
+            i = place + d
+            down_copy(i).wait_recv()
+
+            @pl.when(inner_down)
+            def _():
+                down_copy(i).start()
+
+            cross_copy(i, lane).start()
+            af_copy(2 * i + lane).start()
+
+    @each(places)
     def _(i):
-        ad_wait(i).wait_recv()
-        af_copy(i).start()
+        cross_copy(i, 1 - lane).wait_recv()
+        af_copy(2 * i + 1 - lane).start()
 
     @each(groups)
-    def _(i):
-        af_copy(i).wait_recv()
-
-    span = slots * rank
+    def _(g):
+        af_copy(g).wait_recv()
+
     bg_sel[...] = jnp.zeros_like(bg_sel)
     bu_sel[...] = jnp.zeros_like(bu_sel)
-    mine = pl.ds(pl.multiple_of(half * hwidth, hwidth), hwidth)
-    other = pl.ds(pl.multiple_of((1 - half) * hwidth, hwidth), hwidth)
-    per = prow // owned
+    column = lax.broadcasted_iota(jnp.int32, (1, 2 * span), 1)
+    column = jnp.where(column < span, column, column - span)
+    low = jnp.zeros((1, 2 * span), jnp.int32)
+    high = jnp.zeros((1, 2 * span), jnp.int32)
+    total = 0
     for q in range(slots):
-        g = ids_ref[0, q]
+        own_q = (column >= q * rank) & (column < (q + 1) * rank)
+        low = jnp.where(own_q, total, low)
+        total = total + lengths_ref[q, r]
+        high = jnp.where(own_q, total, high)
+        chosen = chosen_ref[slot_ref[q, r]]
+        g = chosen // owned if owned > 1 else chosen
         at = pl.ds(q * rank, rank)
         at2 = pl.ds(span + q * rank, rank)
-        row0 = ids_ref[1, q] * per if owned > 1 else 0
+        row0 = lax.rem(chosen, owned) * per if owned > 1 else 0
         for dst, part in ((mine, maps), (other, maps_sib)):
             a_sel[at, dst] = part[g, pl.ds(row0, rank), 0:hwidth]
             a_sel[at2, dst] = part[g, pl.ds(row0 + rank, rank), 0:hwidth]
@@ -219,11 +285,12 @@
         da = maps[g, pl.ds(row0 + 2 * rank, rank), hwidth : hwidth + inner]
         da_sel[at, :] = da
         da_sel[at2, :] = da
-    for j in (0, 1, 2):
+    for j in range(4):
         w_copies[j].wait()
 
     parts = whole.shape[0]
     f32 = jnp.float32
+    gain_row = gain_ref[...].astype(f32).reshape(1, -1)
 
     def reduce_far(k):
         part_sib(k).wait_recv()
@@ -247,10 +314,10 @@
         scale = lax.rsqrt(squares / (parts * cols) + EPSILON)
         for b in range(parts):
             x = whole[b, here, :].astype(f32)
-            gain = gain_ref[:, b * cols : (b + 1) * cols].astype(f32)
+            gain = gain_row[:, b * cols : (b + 1) * cols]
             normed[:, b * cols : (b + 1) * cols] = (x * scale * gain).astype(jnp.bfloat16)
         at = lax.broadcasted_iota(jnp.int32, (rc, 2 * span), 0) + k * rc
-        live = (at >= low_ref[...]) & (at < high_ref[...])
+        live = (at >= low) & (at < high)
         low_rank = lax.dot_general(normed[...], a_sel[...], NT, preferred_element_type=f32)
         low_rank = jnp.where(live, low_rank, 0.0).astype(jnp.bfloat16)
         for n0 in range(0, inner, 256):
@@ -284,7 +351,6 @@
         own_part[k, 1] = part_of(m)
 
     reduce_far(CHUNKS - 1)
-    total = total_ref[0]
 
     @each(CHUNKS)
     def _(k):
@@ -304,13 +370,21 @@
         part_sib(k).wait_send()
         part_far(k).wait_send()
 
-    @each(groups, 1)
+    @each(places)
     def _(i):
-        ad_copy(i).wait_send()
+        cross_copy(i, lane).wait_send()
+
+        @pl.when(inner_up & (i <= place))
+        def _():
+            up_copy(i).wait_send()
+
+        @pl.when(inner_down & (i >= place))
+        def _():
+            down_copy(i).wait_send()
 
     @each(groups)
-    def _(i):
-        af_copy(i).wait_send()
+    def _(g):
+        af_copy(g).wait_send()
 
 
 def on_device(
@@ -328,8 +402,6 @@
     selected,
 ):
     groups = lax.axis_size("req")
-    r = lax.axis_index("req")
-    m = lax.axis_index("mlp")
     parts = lax.axis_size("mlp")
     rows, cols = tokens.shape
     owned, rank, width = down_output_maps.shape
@@ -337,29 +409,8 @@
     slots = lengths.shape[1]
     span = slots * rank
     hwidth = width // 2
+    packed = (owned * 3 * rank, hwidth + inner)
     bf16 = jnp.bfloat16
-
-    shared = jnp.concatenate(
-        [jnp.swapaxes(gate_up_input_maps, 1, 2), down_output_maps], axis=1
-    )
-    shared = lax.dynamic_slice_in_dim(shared, (m % 2) * hwidth, hwidth, axis=2)
-    own = jnp.concatenate(
-        [
-            gate_up_output_maps.reshape(owned, 2 * rank, inner),
-            jnp.swapaxes(down_input_maps, 1, 2),
-        ],
-        axis=1,
-    )
-    pack = jnp.concatenate([shared, own], axis=2).reshape(owned * 3 * rank, hwidth + inner)
-
-    lens = lengths[r]
-    ends = jnp.cumsum(lens)
-    starts = ends - lens
-    ids = selected[request_adapter_slot[r]]
-    ids = jnp.stack([ids // owned, ids % owned]).astype(jnp.int32)
-    low = jnp.tile(jnp.repeat(starts, rank), 2).reshape(1, 2 * span)
-    high = jnp.tile(jnp.repeat(ends, rank), 2).reshape(1, 2 * span)
-    total = ends[slots - 1 :]
 
     rc = rows // CHUNKS
     vm, sm, hbm = (
@@ -369,7 +420,7 @@
     return pl.pallas_call(
         functools.partial(kernel, groups, owned, rank, slots),
         out_shape=jax.ShapeDtypeStruct((rows, cols), tokens.dtype),
-        in_specs=[sm, sm, hbm, vm, hbm, hbm, hbm, hbm, vm, vm],
+        in_specs=[sm, sm, sm, hbm, vm] + [hbm] * 7,
         out_specs=vm,
         scratch_shapes=[
             pltpu.VMEM((width, inner), bf16),
@@ -378,8 +429,8 @@
             pltpu.VMEM((parts, rows, cols), bf16),
             pltpu.VMEM((rc, width), bf16),
             pltpu.VMEM((rc, inner), bf16),
-            pltpu.VMEM((groups,) + pack.shape, bf16),
-            pltpu.VMEM((groups, pack.shape[0], hwidth), bf16),
+            pltpu.VMEM((groups,) + packed, bf16),
+            pltpu.VMEM((groups, packed[0], hwidth), bf16),
             pltpu.VMEM((2 * span, width), bf16),
             pltpu.VMEM((2 * span, inner), bf16),
             pltpu.VMEM((2 * span, inner), bf16),
@@ -390,27 +441,32 @@
             pltpu.VMEM((CHUNKS, 2, rc, cols), bf16),
             pltpu.VMEM((CHUNKS, rc, cols), bf16),
             pltpu.VMEM((CHUNKS, rc, cols), bf16),
-            dma((groups,)),
-            dma((groups,)),
+            dma((groups // 2,)),
+            dma((groups // 2,)),
+            dma((groups // 2,)),
+            dma((groups // 2,)),
+            dma((groups // 2,)),
             dma((groups,)),
             dma((groups,)),
         ]
         + [dma((CHUNKS,)) for _ in range(10)]
-        + [dma((5,))],
+        + [dma((4 + 4 * owned,))],
         compiler_params=pltpu.CompilerParams(
             collective_id=0, has_side_effects=True, vmem_limit_bytes=60 * 1024 * 1024
         ),
     )(
-        ids,
-        total,
+        lengths.T,
+        request_adapter_slot.T,
+        selected,
         tokens,
-        norm_gain_vector.reshape(1, width),
+        norm_gain_vector,
         gate_weight,
         up_weight,
         down_weight,
-        pack,
-        low,
-        high,
+        jnp.swapaxes(gate_up_input_maps, 1, 2),
+        gate_up_output_maps.reshape(owned, 2 * rank, inner),
+        jnp.swapaxes(down_input_maps, 1, 2),
+        down_output_maps,
     )
 
 

time: 89.9 us -> 69.6 us (0.77)
  the two profiles are of different devices: /device:TPU:11 before, /device:TPU:0 now
where the time goes in v2:
time: 69.6 us; the launch traced here: 69.5 us
  Pallas kernels  67.2 us (97%)
  local copies, waits for them, and re-layouts  2.26 us (3%)
    pallas_call x1, Pallas kernels, on_device(): pl.pallas_call(functools.partial(kernel, groups, owned, rank, slots), out...  67.2 us
    unnamed x1, local copies, waits for them, and re-layouts  2.26 us

profile of v2, /device:TPU:0, one launch (start us, length us, event | category | flops | bytes accessed | tf_op | source)
XLA Modules:
  0.0 69.5 jit_solution(9838755208399701327)
XLA Ops:
  0.0 67.2 %shard_map.118 = bf16[1024,512]{1,0:T(8,128)(2,1)} custom-call(s32[4,8]{1,0:T(4,128)} %bitcast.8, s32[4,8]{1,0:T(4,128)} %bitcast.9, s32[8]{0:T(128)} %chosen_ref.1, bf16[1024,512]{1,0:T(8,128)(2,1)} %tokens_ref.1, bf16[2048]{0:T(1024)(128)(2,1)} %gain_ref.1, bf16[2048,896]{1,0:T(8,128)(2,1)} %gate_ref.1, bf16[2048,896]{1,0:T(8,128)(2,1)} %up_ref.1, ...), custom_call_target="tpu_custom_call" | custom-call | tf_op jit(solution)/shard_map/pallas_call | solution.py:420
  67.2 2.3 %copy.14 = bf16[1024,512]{1,0:T(8,128)(2,1)} copy(bf16[1024,512]{1,0:T(8,128)(2,1)} %shard_map.118) | data formatting | bytes 2097152

commit v3 on v2

--- a/solution.py
+++ b/solution.py
@@ -36,6 +36,8 @@
     down_v,
     whole,
     normed,
+    gate_sum,
+    up_sum,
     hidden,
     maps,
     maps_sib,
@@ -220,10 +222,12 @@
 
     for j in (3, 0, 1, 2):
         w_copies[j].start()
-    pass_on(0)
-
-    @each(places, 1)
-    def _(d):
+    parts = whole.shape[0]
+    f32 = jnp.float32
+    gain_row = gain_ref[...].astype(f32).reshape(1, -1)
+    early = CHUNKS - 1
+
+    def relay(d, carry):
         @pl.when(place - d >= 0)
         def _():
             i = place - d
@@ -247,6 +251,43 @@
 
             cross_copy(i, lane).start()
             af_copy(2 * i + lane).start()
+
+        return carry
+
+    def base(k):
+        here = rows_of(k)
+        tok_sib(k, sib).wait_recv()
+        tok_fwd(k, diag).wait_recv()
+        squares = jnp.zeros((rc, 1), f32)
+        for b in range(parts):
+            x = whole[b, here, :].astype(f32)
+            squares += jnp.sum(x * x, axis=1, keepdims=True)
+        scale = lax.rsqrt(squares / (parts * cols) + EPSILON)
+        for b in range(parts):
+            x = whole[b, here, :].astype(f32)
+            gain = gain_row[:, b * cols : (b + 1) * cols]
+            normed[k, :, b * cols : (b + 1) * cols] = (x * scale * gain).astype(jnp.bfloat16)
+        for n0 in range(0, inner, 256):
+            n1 = min(n0 + 256, inner)
+            gate_sum[k, :, n0:n1] = jnp.dot(
+                normed[k], gate_v[:, n0:n1], preferred_element_type=f32
+            )
+            up_sum[k, :, n0:n1] = jnp.dot(normed[k], up_v[:, n0:n1], preferred_element_type=f32)
+
+    for copy in w_copies:
+        copy.wait()
+    pass_on(0)
+
+    @each(early)
+    def _(j):
+        first = 1 + (places - 1) * j // early
+        last = 1 + (places - 1) * (j + 1) // early
+        lax.fori_loop(first, last, relay, 0)
+        base(j)
+
+        @pl.when(j < early - 1)
+        def _():
+            pass_on(j + 1)
 
     @each(places)
     def _(i):
@@ -285,13 +326,6 @@
         da = maps[g, pl.ds(row0 + 2 * rank, rank), hwidth : hwidth + inner]
         da_sel[at, :] = da
         da_sel[at2, :] = da
-    for j in range(4):
-        w_copies[j].wait()
-
-    parts = whole.shape[0]
-    f32 = jnp.float32
-    gain_row = gain_ref[...].astype(f32).reshape(1, -1)
-
     def reduce_far(k):
         part_sib(k).wait_recv()
         far_out[k] = (own_part[k, 0] + sib_in[k, 0].astype(f32)).astype(jnp.bfloat16)
@@ -299,32 +333,19 @@
 
     @each(CHUNKS)
     def _(k):
-        here = rows_of(k)
-
-        @pl.when(k < CHUNKS - 1)
-        def _():
-            pass_on(k + 1)
-
-        tok_sib(k, sib).wait_recv()
-        tok_fwd(k, diag).wait_recv()
-        squares = jnp.zeros((rc, 1), f32)
-        for b in range(parts):
-            x = whole[b, here, :].astype(f32)
-            squares += jnp.sum(x * x, axis=1, keepdims=True)
-        scale = lax.rsqrt(squares / (parts * cols) + EPSILON)
-        for b in range(parts):
-            x = whole[b, here, :].astype(f32)
-            gain = gain_row[:, b * cols : (b + 1) * cols]
-            normed[:, b * cols : (b + 1) * cols] = (x * scale * gain).astype(jnp.bfloat16)
+        @pl.when(k == 1)
+        def _():
+            base(early)
+
         at = lax.broadcasted_iota(jnp.int32, (rc, 2 * span), 0) + k * rc
         live = (at >= low) & (at < high)
-        low_rank = lax.dot_general(normed[...], a_sel[...], NT, preferred_element_type=f32)
+        low_rank = lax.dot_general(normed[k], a_sel[...], NT, preferred_element_type=f32)
         low_rank = jnp.where(live, low_rank, 0.0).astype(jnp.bfloat16)
         for n0 in range(0, inner, 256):
             n1 = min(n0 + 256, inner)
-            g = jnp.dot(normed[...], gate_v[:, n0:n1], preferred_element_type=f32)
+            g = gate_sum[k, :, n0:n1]
             g += jnp.dot(low_rank, bg_sel[:, n0:n1], preferred_element_type=f32)
-            u = jnp.dot(normed[...], up_v[:, n0:n1], preferred_element_type=f32)
+            u = up_sum[k, :, n0:n1]
             u += jnp.dot(low_rank, bu_sel[:, n0:n1], preferred_element_type=f32)
             hidden[:, n0:n1] = (jax.nn.silu(g) * u).astype(jnp.bfloat16)
         down_rank = lax.dot_general(hidden[...], da_sel[...], NT, preferred_element_type=f32)
@@ -342,15 +363,14 @@
         sib_out[k, 0] = part_of(diag).astype(jnp.bfloat16)
         sib_out[k, 1] = part_of(sib).astype(jnp.bfloat16)
         part_sib(k).start()
+
+        @pl.when(k == 0)
+        def _():
+            pass_on(early)
+
         own_part[k, 0] = part_of(far)
-
-        @pl.when(k > 0)
-        def _():
-            reduce_far(k - 1)
-
         own_part[k, 1] = part_of(m)
-
-    reduce_far(CHUNKS - 1)
+        reduce_far(k)
 
     @each(CHUNKS)
     def _(k):
@@ -427,7 +447,9 @@
             pltpu.VMEM((width, inner), bf16),
             pltpu.VMEM((inner, width), bf16),
             pltpu.VMEM((parts, rows, cols), bf16),
-            pltpu.VMEM((rc, width), bf16),
+            pltpu.VMEM((CHUNKS, rc, width), bf16),
+            pltpu.VMEM((CHUNKS, rc, inner), jnp.float32),
+            pltpu.VMEM((CHUNKS, rc, inner), jnp.float32),
             pltpu.VMEM((rc, inner), bf16),
             pltpu.VMEM((groups,) + packed, bf16),
             pltpu.VMEM((groups, packed[0], hwidth), bf16),

time: 69.6 us -> 63.2 us (0.908)
  Pallas kernels: 67.2 us -> 60.8 us
    pallas_call x1, Pallas kernels: 67.2 us -> 60.8 us  [on_device(): pl.pallas_call(functools.partial(kernel, groups, owned, rank, slots), out...]
where the time goes in v3:
time: 63.2 us; the launch traced here: 63.1 us
  Pallas kernels  60.8 us (96%)
  local copies, waits for them, and re-layouts  2.26 us (4%)
    pallas_call x1, Pallas kernels, on_device(): pl.pallas_call(functools.partial(kernel, groups, owned, rank, slots), out...  60.8 us
    unnamed x1, local copies, waits for them, and re-layouts  2.26 us

profile of v3, /device:TPU:0, one launch (start us, length us, event | category | flops | bytes accessed | tf_op | source)
XLA Modules:
  0.0 63.1 jit_solution(4399745228285563196)
XLA Ops:
  0.0 60.8 %shard_map.118 = bf16[1024,512]{1,0:T(8,128)(2,1)} custom-call(s32[4,8]{1,0:T(4,128)} %bitcast.8, s32[4,8]{1,0:T(4,128)} %bitcast.9, s32[8]{0:T(128)} %chosen_ref.1, bf16[1024,512]{1,0:T(8,128)(2,1)} %tokens_ref.1, bf16[2048]{0:T(1024)(128)(2,1)} %gain_ref.1, bf16[2048,896]{1,0:T(8,128)(2,1)} %gate_ref.1, bf16[2048,896]{1,0:T(8,128)(2,1)} %up_ref.1, ...), custom_call_target="tpu_custom_call" | custom-call | tf_op jit(solution)/shard_map/pallas_call | solution.py:440
  60.8 2.3 %copy.14 = bf16[1024,512]{1,0:T(8,128)(2,1)} copy(bf16[1024,512]{1,0:T(8,128)(2,1)} %shard_map.118) | data formatting | bytes 2097152

commit v4 on v3

--- a/solution.py
+++ b/solution.py
@@ -333,7 +333,7 @@
 
     @each(CHUNKS)
     def _(k):
-        @pl.when(k == 1)
+        @pl.when(k == early - 1)
         def _():
             base(early)
 

time: 63.2 us -> 61.9 us (0.979)
  Pallas kernels: 60.8 us -> 59.5 us
    pallas_call x1, Pallas kernels: 60.8 us -> 59.5 us  [on_device(): pl.pallas_call(functools.partial(kernel, groups, owned, rank, slots), out...]
where the time goes in v4:
time: 61.9 us; the launch traced here: 61.7 us
  Pallas kernels  59.5 us (96%)
  local copies, waits for them, and re-layouts  2.26 us (4%)
    pallas_call x1, Pallas kernels, on_device(): pl.pallas_call(functools.partial(kernel, groups, owned, rank, slots), out...  59.5 us
    unnamed x1, local copies, waits for them, and re-layouts  2.26 us

profile of v4, /device:TPU:0, one launch (start us, length us, event | category | flops | bytes accessed | tf_op | source)
XLA Modules:
  0.0 61.7 jit_solution(8038968779948438630)
XLA Ops:
  0.0 59.5 %shard_map.118 = bf16[1024,512]{1,0:T(8,128)(2,1)} custom-call(s32[4,8]{1,0:T(4,128)} %bitcast.8, s32[4,8]{1,0:T(4,128)} %bitcast.9, s32[8]{0:T(128)} %chosen_ref.1, bf16[1024,512]{1,0:T(8,128)(2,1)} %tokens_ref.1, bf16[2048]{0:T(1024)(128)(2,1)} %gain_ref.1, bf16[2048,896]{1,0:T(8,128)(2,1)} %gate_ref.1, bf16[2048,896]{1,0:T(8,128)(2,1)} %up_ref.1, ...), custom_call_target="tpu_custom_call" | custom-call | tf_op jit(solution)/shard_map/pallas_call | solution.py:440
  59.5 2.3 %copy.14 = bf16[1024,512]{1,0:T(8,128)(2,1)} copy(bf16[1024,512]{1,0:T(8,128)(2,1)} %shard_map.118) | data formatting | bytes 2097152
